TPU v7x, 32 devices: a whole 2x2x4 slice. The times are simulated.
32 devices in a mesh: dom: 16 (over z, y, x), chan: 2 (over core).
Axes of the slice: x: 2, y: 2, z: 4, core: 2. Of those that a mesh axis runs over, the one named last changes fastest.
Arguments:
- features: bfloat16 [16384, 512], P('dom', 'chan'), may hold values from -6 to 6
- w_self: bfloat16 [512, 512], P('chan'), may hold values from -0.25 to 0.25
- w_neigh: bfloat16 [512, 512], P('chan'), may hold values from -1.5 to 1.5
- degrees: int32 [16384], P('dom'), may hold values from 16 to 48
- local_src: int32 [128], P('dom'), may hold values from 0 to 7
- local_dst: int32 [128], P('dom'), may hold values from 0 to 7
- local_tiles: bfloat16 [128, 128, 128], P('dom'), may hold values from 0 to 1, as said below
- remote_src: int32 [256], P('dom'), may hold values from 0 to 7
- remote_part: int32 [256, 1], P('dom'), may hold values from 0 to 15; in each aligned block of 16 rows (0 to 15, 16 to 31, ...) at most 2 rows name the same one
- remote_dst: int32 [256], P('dom'), may hold values from 0 to 7
- remote_tiles: bfloat16 [256, 128, 128], P('dom'), may hold values from 0 to 1, as said below
- cotangent: bfloat16 [16384, 512], P('dom', 'chan'), may hold values from -6 to 6
Outputs:
- output: bfloat16 [16384, 512], P('dom', 'chan')
- grad_self: float32 [512, 512], P('chan')
- grad_neigh: float32 [512, 512], P('chan')
- grad_features: bfloat16 [16384, 512], P('dom', 'chan')
Inputs may be any that keep to these rules, and one draw needn't show every extreme that they name: `remote_part`: among the 16 remote tiles of one partition each partition is named at most 2 times, a bound that some block reaches. `local_tiles`: every entry is 0 or 1. `remote_tiles`: every entry is 0 or 1.
All inputs are finite; a program needn't handle non-finite values.
Results may differ from a plain program's by a relative error of at most 0.015.
Values may be sent and summed in bfloat16 or wider, within the bound.
No kernel may reach another device: no remote copies, remote signals or barrier semaphores. Data moves between devices by JAX's collectives and lax.ppermute only.
A program may use at most 64 MiB of HBM per device.

v0:
```python
import math
import jax
import jax.numpy as jnp
from jax import lax
from jax.sharding import PartitionSpec as P

TILE = 128
CAP = 2


def silu_slope(value):
    sig = jax.nn.sigmoid(value)
    return sig * (1.0 + value * (1.0 - sig))


def tile_products(tiles, sources, feat_blocks):
    picked = jnp.take(feat_blocks, sources, axis=0)
    return jnp.einsum("tij,tic->tjc", tiles, picked, preferred_element_type=jnp.float32)


def local_sum(local_tiles, local_src, local_dst, feat_blocks, block_count):
    terms = tile_products(local_tiles, local_src, feat_blocks)
    onehot = (jnp.arange(block_count, dtype=jnp.int32)[:, None] == local_dst[None, :]).astype(
        jnp.float32
    )
    flat = terms.reshape(terms.shape[0], -1)
    return jnp.einsum("bt,tk->bk", onehot, flat, precision=lax.Precision.HIGHEST)


def push_partials(outgoing, out_blocks):
    return (
        lax.all_to_all(outgoing, "dom", split_axis=0, concat_axis=0, tiled=True),
        lax.all_to_all(out_blocks, "dom", split_axis=0, concat_axis=0, tiled=True),
    )


def per_device(
    features,
    w_self,
    w_neigh,
    degrees,
    local_src,
    local_dst,
    local_tiles,
    remote_src,
    remote_part,
    remote_dst,
    remote_tiles,
    cotangent,
):
    domains = lax.axis_size("dom")
    node_rows, channels = features.shape
    block_count = node_rows // TILE
    remote_count = remote_tiles.shape[0]
    slot_count = domains * CAP
    feat_blocks = features.reshape(block_count, TILE, channels)
    targets = remote_part[:, 0]
    counter = jnp.arange(remote_count, dtype=jnp.int32)
    same_before = (targets[:, None] == targets[None, :]) & (counter[None, :] < counter[:, None])
    position = jnp.sum(jnp.where(same_before, 1, 0), axis=1).astype(jnp.int32)
    slot_index = targets * CAP + position
    local_part = local_sum(local_tiles, local_src, local_dst, feat_blocks, block_count)
    pushed = tile_products(remote_tiles, remote_src, feat_blocks).astype(jnp.bfloat16)
    outgoing = jnp.zeros((slot_count, TILE * channels), jnp.bfloat16)
    outgoing = outgoing.at[slot_index].set(pushed.reshape(remote_count, TILE * channels))
    out_blocks = jnp.zeros((slot_count,), jnp.int32).at[slot_index].set(remote_dst)
    received, got_blocks = push_partials(
        outgoing.reshape(domains, CAP * TILE * channels), out_blocks.reshape(domains, CAP)
    )
    incoming = received.reshape(slot_count, TILE * channels)
    got_index = got_blocks.reshape(slot_count)
    onehot_in = (jnp.arange(block_count, dtype=jnp.int32)[:, None] == got_index[None, :]).astype(
        jnp.bfloat16
    )
    remote_part_sum = jnp.dot(onehot_in, incoming, preferred_element_type=jnp.float32)
    summed = (local_part + remote_part_sum).reshape(node_rows, channels)
    divisor = degrees.astype(jnp.float32)[:, None]
    averaged = (summed / divisor).astype(jnp.bfloat16)
    joined = jnp.concatenate([features, averaged], axis=1)
    weights = jnp.concatenate([w_self, w_neigh], axis=0)
    partial_value = jnp.dot(joined, weights, preferred_element_type=jnp.float32)
    preact = lax.psum_scatter(
        partial_value.astype(jnp.bfloat16), "chan", scatter_dimension=1, tiled=True
    ).astype(jnp.float32)
    output = jax.nn.silu(preact).astype(jnp.bfloat16)
    slopes_own = (cotangent.astype(jnp.float32) * silu_slope(preact)).astype(jnp.bfloat16)
    slopes_all = lax.all_gather(slopes_own, "chan", axis=1, tiled=True)
    grad_terms = lax.dot_general(
        joined, slopes_all, (((0,), (0,)), ((), ())), preferred_element_type=jnp.float32
    )
    grad_sums = lax.psum(grad_terms, "dom") * (1.0 / math.sqrt(float(node_rows * domains)))
    grad_self = grad_sums[:channels]
    grad_neigh = grad_sums[channels:]
    backward = lax.dot_general(
        slopes_all, weights, (((1,), (1,)), ((), ())), preferred_element_type=jnp.float32
    )
    back_self = backward[:, :channels]
    back_rows = (backward[:, channels:] / divisor).astype(jnp.bfloat16)
    back_blocks = back_rows.reshape(block_count, TILE, channels)
    returning = jnp.take(back_blocks.reshape(block_count, TILE * channels), got_index, axis=0)
    returned = lax.all_to_all(
        returning.reshape(domains, CAP * TILE * channels),
        "dom",
        split_axis=0,
        concat_axis=0,
        tiled=True,
    )
    returned = returned.reshape(slot_count, TILE, channels)
    remote_rows = jnp.take(returned, slot_index, axis=0)
    remote_terms = jnp.einsum(
        "tij,tjc->tic", remote_tiles, remote_rows, preferred_element_type=jnp.float32
    )
    onehot_remote = (
        jnp.arange(block_count, dtype=jnp.int32)[:, None] == remote_src[None, :]
    ).astype(jnp.float32)
    remote_back = jnp.einsum(
        "bt,tk->bk",
        onehot_remote,
        remote_terms.reshape(remote_count, -1),
        precision=lax.Precision.HIGHEST,
    )
    local_rows = jnp.take(back_blocks, local_dst, axis=0)
    local_terms = jnp.einsum(
        "tij,tjc->tic", local_tiles, local_rows, preferred_element_type=jnp.float32
    )
    onehot_local = (jnp.arange(block_count, dtype=jnp.int32)[:, None] == local_src[None, :]).astype(
        jnp.float32
    )
    local_back = jnp.einsum(
        "bt,tk->bk",
        onehot_local,
        local_terms.reshape(local_terms.shape[0], -1),
        precision=lax.Precision.HIGHEST,
    )
    gathered = (remote_back + local_back).reshape(node_rows, channels)
    grad_features = (back_self + gathered).astype(jnp.bfloat16)
    return (output, grad_self, grad_neigh, grad_features)


def solution(mesh):
    in_specs = (
        P("dom", "chan"),
        P("chan", None),
        P("chan", None),
        P("dom"),
        P("dom"),
        P("dom"),
        P("dom", None, None),
        P("dom"),
        P("dom", None),
        P("dom"),
        P("dom", None, None),
        P("dom", "chan"),
    )
    out_specs = (P("dom", "chan"), P("chan", None), P("chan", None), P("dom", "chan"))
    return jax.shard_map(
        per_device, mesh=mesh, in_specs=in_specs, out_specs=out_specs, check_vma=False
    )
```

profile of v0, /device:TPU:0, one launch (start us, length us, event | category | flops | bytes accessed | tf_op | source)
XLA Modules:
  0.0 361.2 jit_solution(5732093317905515113)
XLA Ops:
  7.2 0.9 select_reduce_fusion
  8.1 0.7 and_bitcast_fusion
  8.8 0.8 scatter_custom_fusion
  9.5 0.7 all_to_all.16
  10.2 8.3 %all-to-all-start = ((s32[16,1,2]{2,1,0:T(1,128)}), s32[16,1,2]{2,1,0:T(1,128)S(1)}, u32[]{:S(2)}, u32[]{:S(2)}) async-start(s32[16,1,2]{2,1,0:T(1,128)} %bitcast.5), calls=%async_computation | async-start | bytes 16384 | tf_op jit(solution)/shard_map/all_to_all | solution.py:33
  18.6 0.7 compare_select_fusion.4
  19.2 0.7 compare_and_fusion.3
  19.9 5.9 %all-to-all-done = s32[16,1,2]{2,1,0:T(1,128)S(1)} async-done(((s32[16,1,2]{2,1,0:T(1,128)}), s32[16,1,2]{2,1,0:T(1,128)S(1)}, u32[]{:S(2)}, u32[]{:S(2)}) %all-to-all-start) | async-done | bytes 160 | tf_op jit(solution)/shard_map/all_to_all | solution.py:33
  25.9 1.7 gather_fusion
  27.6 0.6 fusion
  28.1 1.7 copy.71
  29.8 3.4 scatter_custom_fusion.1
  33.2 4.4 %all_to_all.21 = bf16[16,1,65536]{2,1,0:T(2,128)(2,1)} reshape(bf16[32,32768]{1,0:T(8,128)(2,1)S(1)} %scatter_custom_fusion.1) | data formatting | bytes 4194304 | tf_op jit(solution)/shard_map/all_to_all | solution.py:32
  38.0 12.9 %reduce.8 = bf16[16,65536]{1,0:T(8,128)(2,1)S(1)} reduce(bf16[16,1,65536]{2,1,0:T(2,128)(2,1)} %all_to_all.21, bf16[]{:T(256)} %broadcast.165), dimensions={1}, to_apply=%all_to_all.21.reduce_sub_computation | reduce | bytes 4194306 | tf_op jit(solution)/shard_map/all_to_all | solution.py:32
  51.0 2.8 reshape.226
  53.8 3.8 %all-to-all-start.1 = ((bf16[16,2,32768]{2,1,0:T(2,128)(2,1)}), bf16[16,2,32768]{2,1,0:T(2,128)(2,1)S(1)}, u32[]{:S(2)}, u32[]{:S(2)}) async-start(bf16[16,2,32768]{2,1,0:T(2,128)(2,1)} %reshape.226), calls=%async_computation.1 | async-start | bytes 4194304 | tf_op jit(solution)/shard_map/all_to_all | solution.py:32
  57.9 1.4 gather_fusion.3
  59.3 2.4 convolution_bitcast_fusion.2
  61.8 2.6 copy.54
  64.3 1.9 copy.70
  66.2 0.7 constant_dynamic-update-slice_fusion.1
  67.0 0.7 constant_dynamic-update-slice_fusion
  67.7 1.6 fusion.27
  69.2 0.5 broadcast.161
  69.8 0.7 reduce.7
  70.5 29.3 %all-to-all-done.1 = bf16[16,2,32768]{2,1,0:T(2,128)(2,1)S(1)} async-done(((bf16[16,2,32768]{2,1,0:T(2,128)(2,1)}), bf16[16,2,32768]{2,1,0:T(2,128)(2,1)S(1)}, u32[]{:S(2)}, u32[]{:S(2)}) %all-to-all-start.1) | async-done | bytes 2097184 | tf_op jit(solution)/shard_map/all_to_all | solution.py:32
  99.9 6.7 %reshape.227 = bf16[16,1,65536]{2,1,0:T(2,128)(2,1)} reshape(bf16[16,2,32768]{2,1,0:T(2,128)(2,1)S(1)} %all-to-all-done.1) | data formatting | bytes 4194304
  106.6 12.4 %reduce.1 = bf16[16,65536]{1,0:T(8,128)(2,1)S(1)} reduce(bf16[16,1,65536]{2,1,0:T(2,128)(2,1)} %reshape.227, bf16[]{:T(256)} %constant.72), dimensions={1}, to_apply=%all_to_all.19.reduce_sub_computation | reduce | bytes 4194306 | tf_op jit(solution)/shard_map/all_to_all | solution.py:32
  119.0 1.9 reshape.137
  120.8 2.2 convolution_add_fusion.1
  123.5 0.8 copy-done.8
  124.3 2.8 convolution_convert_fusion
  127.3 12.4 %reduce-scatter.2.cloned.1.call-done = bf16[1024,256]{1,0:T(8,128)(2,1)} async-done(((bf16[1024,512]{1,0:T(8,128)(2,1)}), bf16[1024,256]{1,0:T(8,128)(2,1)}) %reduce-scatter.2.cloned.1.call-update) | async-done | bytes 524304 | tf_op jit(solution)/shard_map/reduce_scatter | solution.py:82
  139.7 2.5 fusion.8
  142.4 1.2 broadcast_in_dim.80
  143.6 3.9 %broadcast_in_dim.81 = pred[16,1,65536]{2,0,1:T(8,128)(4,1)} reshape(pred[16,2,32768]{2,1,0:T(4,128)(4,1)S(1)} %broadcast_in_dim.80) | data formatting | bytes 2097152 | tf_op jit(solution)/shard_map/jit(_take)/broadcast_in_dim | solution.py:100
  147.5 4.8 %all-gather.2.cloned.1.call-done = bf16[1024,512]{1,0:T(8,128)(2,1)} async-done(((bf16[1024,256]{1,0:T(8,128)(2,1)}), bf16[1024,512]{1,0:T(8,128)(2,1)}) %all-gather.2.cloned.1.call-update) | async-done | bytes 1048592 | tf_op jit(solution)/shard_map/all_gather | solution.py:87
  152.4 2.1 fusion.43
  154.5 1.3 copy-done.1
  156.3 0.5 copy-done.5
  156.8 1.9 gather_fusion.1
  158.7 1.9 gather.19
  160.6 2.2 broadcast_select_fusion
  162.8 2.8 reduce.9
  165.6 4.0 %reshape.228 = bf16[16,2,32768]{2,1,0:T(2,128)(2,1)} reshape(bf16[16,65536]{1,0:T(8,128)(2,1)} %reduce.9) | data formatting | bytes 4194304
  169.6 7.0 %all-to-all-start.2 = ((bf16[16,2,32768]{2,1,0:T(2,128)(2,1)}), bf16[16,2,32768]{2,1,0:T(2,128)(2,1)S(1)}, u32[]{:S(2)}, u32[]{:S(2)}) async-start(bf16[16,2,32768]{2,1,0:T(2,128)(2,1)} %reshape.228), calls=%async_computation.3 | async-start | bytes 4194304 | tf_op jit(solution)/shard_map/all_to_all | solution.py:101
  176.9 3.1 fusion.17
  180.1 1.6 gather_fusion.4
  181.7 1.4 convolution_bitcast_fusion.1
  183.1 2.6 copy.65
  185.7 2.8 copy.73
  188.5 127.0 %all-reduce.2.cloned.1.call-done = f32[512,512]{1,0:T(8,128)} async-done(((f32[512,512]{1,0:T(8,128)}), f32[512,512]{1,0:T(8,128)}) %all-reduce.2.cloned.1.call-update) | async-done | bytes 1048592 | tf_op jit(solution)/shard_map/psum | solution.py:91
  315.5 1.3 broadcast_multiply_fusion
  316.9 1.0 fusion.42
  317.9 6.7 %reshape.229 = bf16[16,1,65536]{2,1,0:T(2,128)(2,1)} reshape(bf16[16,2,32768]{2,1,0:T(2,128)(2,1)S(1)} %all-to-all-done.2) | data formatting | bytes 4194304
  324.6 12.4 %reduce.3 = bf16[16,65536]{1,0:T(8,128)(2,1)S(1)} reduce(bf16[16,1,65536]{2,1,0:T(2,128)(2,1)} %reshape.229, bf16[]{:T(256)} %constant.72), dimensions={1}, to_apply=%all_to_all.20.reduce_sub_computation | reduce | bytes 4194306 | tf_op jit(solution)/shard_map/all_to_all | solution.py:101
  337.0 2.0 reshape.140
  339.0 3.2 gather_fusion.2
  342.2 1.8 convolution_bitcast_fusion
  344.0 2.0 copy.72
  346.0 2.5 fusion.28
  348.5 1.6 convolution_add_fusion
  350.2 2.3 reshape.144
  352.5 2.2 fusion.10
  (55 shorter events, 2.6 us)
Async XLA Ops:
  7.2 20.4 %copy-start = (bf16[16,128,128]{2,1,0:T(8,128)(2,1)S(1)}, bf16[16,128,128]{2,1,0:T(8,128)(2,1)}, u32[]{:S(2)}) copy-start(bf16[16,128,128]{2,1,0:T(8,128)(2,1)} %param.24) | copy-start | bytes 1572868
  10.2 15.6 %all-to-all-start = ((s32[16,1,2]{2,1,0:T(1,128)}), s32[16,1,2]{2,1,0:T(1,128)S(1)}, u32[]{:S(2)}, u32[]{:S(2)}) async-start(s32[16,1,2]{2,1,0:T(1,128)} %bitcast.5), calls=%async_computation | async-start | bytes 16384 | tf_op jit(solution)/shard_map/all_to_all | solution.py:33
  53.8 4.1 %copy-start.15 = (s32[8]{0:T(128)S(1)}, s32[8]{0:T(128)}, u32[]{:S(2)}) copy-start(s32[8]{0:T(128)} %param.18) | copy-start | bytes 100
  53.8 4.1 %copy-start.3 = (bf16[1024,256]{1,0:T(8,128)(2,1)S(1)}, bf16[1024,256]{1,0:T(8,128)(2,1)}, u32[]{:S(2)}) copy-start(bf16[1024,256]{1,0:T(8,128)(2,1)} %param.14) | copy-start | bytes 1572868
  53.8 5.5 %copy-start.7 = (bf16[8,128,128]{2,1,0:T(8,128)(2,1)S(1)}, bf16[8,128,128]{2,1,0:T(8,128)(2,1)}, u32[]{:S(2)}) copy-start(bf16[8,128,128]{2,1,0:T(8,128)(2,1)} %param.20) | copy-start | bytes 786436
  53.8 46.1 %all-to-all-start.1 = ((bf16[16,2,32768]{2,1,0:T(2,128)(2,1)}), bf16[16,2,32768]{2,1,0:T(2,128)(2,1)S(1)}, u32[]{:S(2)}, u32[]{:S(2)}) async-start(bf16[16,2,32768]{2,1,0:T(2,128)(2,1)} %reshape.226), calls=%async_computation.1 | async-start | bytes 4194304 | tf_op jit(solution)/shard_map/all_to_all | solution.py:32
  57.6 82.1 %reduce-scatter.2.cloned.1.call-start = ((), (), s32[]{:S(2)}) async-start(), calls=%async_computation.4 | async-start | bytes 1572864 | tf_op jit(solution)/shard_map/reduce_scatter | solution.py:82
  61.8 4.5 %copy-start.12 = (s32[1024]{0:T(1024)S(1)}, s32[1024]{0:T(1024)}, u32[]{:S(2)}) copy-start(s32[1024]{0:T(1024)} %param.17) | copy-start | bytes 12292
  64.3 1.9 copy-start.10
  64.3 2.7 copy-start.11
  64.3 3.4 copy-start.13
  123.5 0.8 copy-start.8
  124.3 15.5 %copy-start.9 = (bf16[1024,256]{1,0:T(8,128)(2,1)S(1)}, bf16[1024,256]{1,0:T(8,128)(2,1)}, u32[]{:S(2)}) copy-start(bf16[1024,256]{1,0:T(8,128)(2,1)} %param.25) | copy-start | bytes 1572868
  127.1 25.3 %all-gather.2.cloned.1.call-start = ((), (), s32[]{:S(2)}) async-start(), calls=%async_computation.5 | async-start | bytes 1572864 | tf_op jit(solution)/shard_map/all_gather | solution.py:87
  154.5 1.3 copy-start.1
  156.0 0.8 copy-start.5
  169.6 7.3 %copy-start.4 = (bf16[1024,256]{1,0:T(8,128)(2,1)S(1)}, bf16[1024,256]{1,0:T(8,128)(2,1)}, u32[]{:S(2)}) copy-start(bf16[1024,256]{1,0:T(8,128)(2,1)} %param.14) | copy-start | bytes 1572868
  169.6 148.3 %all-to-all-start.2 = ((bf16[16,2,32768]{2,1,0:T(2,128)(2,1)}), bf16[16,2,32768]{2,1,0:T(2,128)(2,1)S(1)}, u32[]{:S(2)}, u32[]{:S(2)}) async-start(bf16[16,2,32768]{2,1,0:T(2,128)(2,1)} %reshape.228), calls=%async_computation.3 | async-start | bytes 4194304 | tf_op jit(solution)/shard_map/all_to_all | solution.py:101
  176.6 139.0 %all-reduce.2.cloned.1.call-start = ((), (), s32[]{:S(2)}) async-start(), calls=%async_computation.6 | async-start | bytes 2097152 | tf_op jit(solution)/shard_map/psum | solution.py:91
  344.0 2.0 copy-start.14
  346.0 2.5 copy-start.6
  348.5 4.0 %copy-start.2 = (f32[1024,512]{1,0:T(8,128)S(1)}, f32[1024,512]{1,0:T(8,128)}, u32[]{:S(2)}) copy-start(f32[1024,512]{1,0:T(8,128)} %copy-done.1) | copy-start | bytes 6291460
Sparse Core Ops, SparseCore 0:
  127.2 12.4 reduce-scatter.1
  142.4 9.9 all-gather.1
  182.6 132.8 all-reduce.1
where the time goes:
time: 362 us; the launch traced here: 361 us
  waiting for transfers between devices  180 us (50%)
  local copies, waits for them, and re-layouts  72.9 us (20%)
  other arithmetic  52.6 us (15%)
  matrix products  22.1 us (6%)
  starting transfers between devices  19.9 us (5%)
  between operations  14.1 us (4%)
    psum x1, waiting for transfers between devices, per_device(): lax.psum(grad_terms, 'dom') * (1.0 / math.sqrt(float(node_rows * domains)))  127 us
    unnamed x41, local copies, waits for them, and re-layouts  32.2 us
    all_to_all x1, waiting for transfers between devices, push_partials(): lax.all_to_all(outgoing, 'dom', split_axis=0, concat_axis=0, tiled=True)  29.3 us
    all_to_all x2, other arithmetic, push_partials(): lax.all_to_all(outgoing, 'dom', split_axis=0, concat_axis=0, tiled=True)  25.3 us
    reduce_scatter x1, waiting for transfers between devices, per_device(): lax.psum_scatter(partial_value.astype(jnp.bfloat16), 'chan', scatter_dime...  12.4 us
    all_to_all x1, other arithmetic, per_device(): lax.all_to_all(returning.reshape(domains, CAP * TILE * channels), 'dom',...  12.4 us
    all_to_all x1, starting transfers between devices, push_partials(): lax.all_to_all(out_blocks, 'dom', split_axis=0, concat_axis=0, tiled=True)  8.34 us
  transfers between devices with their start and end apart: 6, of which 5 were waited for; matrix products, arithmetic and copies ran while one was open for 9% of the time, Pallas kernels for 0%

commit v1 on v0

--- a/solution.py
+++ b/solution.py
@@ -88,7 +88,9 @@
     grad_terms = lax.dot_general(
         joined, slopes_all, (((0,), (0,)), ((), ())), preferred_element_type=jnp.float32
     )
-    grad_sums = lax.psum(grad_terms, "dom") * (1.0 / math.sqrt(float(node_rows * domains)))
+    grad_sums = jnp.sum(lax.all_gather(grad_terms, "dom"), axis=0) * (
+        1.0 / math.sqrt(float(node_rows * domains))
+    )
     grad_self = grad_sums[:channels]
     grad_neigh = grad_sums[channels:]
     backward = lax.dot_general(

time: 362 us -> 400 us (1.10)
  waiting for transfers between devices: 180 us -> 211 us
  other arithmetic: 52.6 us -> 59.5 us
    psum x1 -> x0, waiting for transfers between devices: 127 us -> none  [per_device(): lax.psum(grad_terms, 'dom') * (1.0 / math.sqrt(float(node_rows * domains)))]
    all_gather x0 -> x1, waiting for transfers between devices: none -> 97.3 us  [per_device(): lax.all_gather(grad_terms, 'dom')]
    all_to_all x1, waiting for transfers between devices: 0.01 us -> 55.9 us  [per_device(): lax.all_to_all(returning.reshape(domains, CAP * TILE * channels), 'dom',...]
    reduce_sum x0 -> x1, other arithmetic: none -> 7.91 us  [per_device(): jnp.sum(lax.all_gather(grad_terms, 'dom'), axis=0)]
    all_gather x1, waiting for transfers between devices: 4.84 us -> 9.84 us  [per_device(): slopes_all = lax.all_gather(slopes_own, 'chan', axis=1, tiled=True)]
    unnamed x41 -> x39, local copies, waits for them, and re-layouts: 32.2 us -> 31.3 us
  transfers between devices with their start and end apart: 6 -> 6, of which waited for: 5 -> 6; matrix products, arithmetic and copies ran while one was open for 9% -> 20% of each run, Pallas kernels for 0% -> 0%
where the time goes in v1:
time: 400 us; the launch traced here: 399 us
  waiting for transfers between devices  211 us (53%)
  local copies, waits for them, and re-layouts  71.8 us (18%)
  other arithmetic  59.5 us (15%)
  matrix products  23 us (6%)
  starting transfers between devices  19.7 us (5%)
  between operations  14.1 us (4%)
    all_gather x1, waiting for transfers between devices, per_device(): lax.all_gather(grad_terms, 'dom')  97.3 us
    all_to_all x1, waiting for transfers between devices, per_device(): lax.all_to_all(returning.reshape(domains, CAP * TILE * channels), 'dom',...  55.9 us
    unnamed x39, local copies, waits for them, and re-layouts  31.3 us
    all_to_all x1, waiting for transfers between devices, push_partials(): lax.all_to_all(outgoing, 'dom', split_axis=0, concat_axis=0, tiled=True)  29.3 us
    all_to_all x2, other arithmetic, push_partials(): lax.all_to_all(outgoing, 'dom', split_axis=0, concat_axis=0, tiled=True)  25.4 us
    reduce_scatter x1, waiting for transfers between devices, per_device(): lax.psum_scatter(partial_value.astype(jnp.bfloat16), 'chan', scatter_dime...  12.6 us
    all_to_all x1, other arithmetic, per_device(): lax.all_to_all(returning.reshape(domains, CAP * TILE * channels), 'dom',...  12.4 us
    all_gather x1, waiting for transfers between devices, per_device(): slopes_all = lax.all_gather(slopes_own, 'chan', axis=1, tiled=True)  9.84 us
  transfers between devices with their start and end apart: 6, of which 6 were waited for; matrix products, arithmetic and copies ran while one was open for 20% of the time, Pallas kernels for 0%

profile of v1, /device:TPU:0, one launch (start us, length us, event | category | flops | bytes accessed | tf_op | source)
XLA Modules:
  0.0 398.9 jit_solution(18375427595884846191)
XLA Ops:
  7.2 0.9 select_reduce_fusion
  8.1 0.7 and_bitcast_fusion
  8.8 0.8 scatter_custom_fusion
  9.5 0.7 all_to_all.16
  10.2 8.3 %all-to-all-start = ((s32[16,1,2]{2,1,0:T(1,128)}), s32[16,1,2]{2,1,0:T(1,128)S(1)}, u32[]{:S(2)}, u32[]{:S(2)}) async-start(s32[16,1,2]{2,1,0:T(1,128)} %bitcast.5), calls=%async_computation | async-start | bytes 16384 | tf_op jit(solution)/shard_map/all_to_all | solution.py:33
  18.6 0.7 compare_select_fusion.4
  19.2 0.7 compare_and_fusion.3
  19.9 5.9 %all-to-all-done = s32[16,1,2]{2,1,0:T(1,128)S(1)} async-done(((s32[16,1,2]{2,1,0:T(1,128)}), s32[16,1,2]{2,1,0:T(1,128)S(1)}, u32[]{:S(2)}, u32[]{:S(2)}) %all-to-all-start) | async-done | bytes 160 | tf_op jit(solution)/shard_map/all_to_all | solution.py:33
  25.9 1.7 gather_fusion
  27.6 0.6 fusion
  28.1 1.7 copy.71
  29.8 3.4 scatter_custom_fusion.1
  33.2 4.4 %all_to_all.21 = bf16[16,1,65536]{2,1,0:T(2,128)(2,1)} reshape(bf16[32,32768]{1,0:T(8,128)(2,1)S(1)} %scatter_custom_fusion.1) | data formatting | bytes 4194304 | tf_op jit(solution)/shard_map/all_to_all | solution.py:32
  37.5 0.5 broadcast.165
  38.1 13.0 %reduce.8 = bf16[16,65536]{1,0:T(8,128)(2,1)S(1)} reduce(bf16[16,1,65536]{2,1,0:T(2,128)(2,1)} %all_to_all.21, bf16[]{:T(256)} %broadcast.165), dimensions={1}, to_apply=%all_to_all.21.reduce_sub_computation | reduce | bytes 4194306 | tf_op jit(solution)/shard_map/all_to_all | solution.py:32
  51.1 2.8 reshape.227
  53.9 3.8 all-to-all-start.1
  58.0 1.4 gather_fusion.3
  59.4 2.4 convolution_bitcast_fusion.2
  61.9 2.6 copy.54
  64.4 1.9 copy.70
  66.3 0.7 constant_dynamic-update-slice_fusion.1
  67.1 0.7 constant_dynamic-update-slice_fusion
  67.8 1.6 fusion.27
  69.9 0.7 reduce.7
  70.6 29.3 %all-to-all-done.1 = bf16[16,2,32768]{2,1,0:T(2,128)(2,1)S(1)} async-done(((bf16[16,2,32768]{2,1,0:T(2,128)(2,1)}), bf16[16,2,32768]{2,1,0:T(2,128)(2,1)S(1)}, u32[]{:S(2)}, u32[]{:S(2)}) %all-to-all-start.1) | async-done | bytes 2097184 | tf_op jit(solution)/shard_map/all_to_all | solution.py:32
  100.0 6.7 %reshape.228 = bf16[16,1,65536]{2,1,0:T(2,128)(2,1)} reshape(bf16[16,2,32768]{2,1,0:T(2,128)(2,1)S(1)} %all-to-all-done.1) | data formatting | bytes 4194304
  106.6 12.4 %reduce.1 = bf16[16,65536]{1,0:T(8,128)(2,1)S(1)} reduce(bf16[16,1,65536]{2,1,0:T(2,128)(2,1)} %reshape.228, bf16[]{:T(256)} %constant.74), dimensions={1}, to_apply=%all_to_all.19.reduce_sub_computation | reduce | bytes 4194306 | tf_op jit(solution)/shard_map/all_to_all | solution.py:32
  119.0 1.9 reshape.137
  120.9 2.2 convolution_add_fusion.1
  123.5 2.8 convolution_convert_fusion
  126.4 12.6 %reduce-scatter.2.cloned.1.call-done = bf16[1024,256]{1,0:T(8,128)(2,1)} async-done(((bf16[1024,512]{1,0:T(8,128)(2,1)}), bf16[1024,256]{1,0:T(8,128)(2,1)}) %reduce-scatter.2.cloned.1.call-update) | async-done | bytes 524304 | tf_op jit(solution)/shard_map/reduce_scatter | solution.py:82
  139.0 2.5 fusion.8
  141.8 9.8 %all-gather.4.cloned.1.call-done = bf16[1024,512]{1,0:T(8,128)(2,1)} async-done(((bf16[1024,256]{1,0:T(8,128)(2,1)}), bf16[1024,512]{1,0:T(8,128)(2,1)}) %all-gather.4.cloned.1.call-update) | async-done | bytes 1048592 | tf_op jit(solution)/shard_map/all_gather | solution.py:87
  151.6 3.0 fusion.17
  154.8 1.2 broadcast_in_dim.80
  155.9 3.9 broadcast_in_dim.81
  159.9 2.1 fusion.43
  162.0 1.3 copy-done.1
  163.8 0.5 copy-done.4
  164.3 1.9 gather_fusion.1
  166.2 1.9 gather.19
  168.1 2.2 broadcast_select_fusion
  170.3 2.9 reduce.9
  173.2 4.0 %reshape.229 = bf16[16,2,32768]{2,1,0:T(2,128)(2,1)} reshape(bf16[16,65536]{1,0:T(8,128)(2,1)} %reduce.9) | data formatting | bytes 4194304
  177.2 7.0 %all-to-all-start.2 = ((bf16[16,2,32768]{2,1,0:T(2,128)(2,1)}), bf16[16,2,32768]{2,1,0:T(2,128)(2,1)S(1)}, u32[]{:S(2)}, u32[]{:S(2)}) async-start(bf16[16,2,32768]{2,1,0:T(2,128)(2,1)} %reshape.229), calls=%async_computation.3 | async-start | bytes 4194304 | tf_op jit(solution)/shard_map/all_to_all | solution.py:103
  184.2 1.4 gather_fusion.4
  185.6 2.5 convolution_bitcast_fusion.1
  188.1 2.6 copy.65
  190.6 2.8 copy.73
  193.5 55.9 %all-to-all-done.2 = bf16[16,2,32768]{2,1,0:T(2,128)(2,1)S(1)} async-done(((bf16[16,2,32768]{2,1,0:T(2,128)(2,1)}), bf16[16,2,32768]{2,1,0:T(2,128)(2,1)S(1)}, u32[]{:S(2)}, u32[]{:S(2)}) %all-to-all-start.2) | async-done | bytes 2097184 | tf_op jit(solution)/shard_map/all_to_all | solution.py:103
  249.3 6.7 %reshape.230 = bf16[16,1,65536]{2,1,0:T(2,128)(2,1)} reshape(bf16[16,2,32768]{2,1,0:T(2,128)(2,1)S(1)} %all-to-all-done.2) | data formatting | bytes 4194304
  256.0 12.4 %reduce.3 = bf16[16,65536]{1,0:T(8,128)(2,1)S(1)} reduce(bf16[16,1,65536]{2,1,0:T(2,128)(2,1)} %reshape.230, bf16[]{:T(256)} %constant.74), dimensions={1}, to_apply=%all_to_all.20.reduce_sub_computation | reduce | bytes 4194306 | tf_op jit(solution)/shard_map/all_to_all | solution.py:103
  268.4 2.0 reshape.140
  270.4 3.2 gather_fusion.2
  273.6 1.8 convolution_bitcast_fusion
  275.4 2.0 copy.72
  277.4 2.5 fusion.28
  279.9 1.6 convolution_add_fusion
  281.5 2.4 reshape.144
  283.9 2.2 fusion.10
  286.0 97.3 %all-gather.6.cloned.1.call-done = f32[8192,512]{1,0:T(8,128)} async-done(((f32[512,512]{1,0:T(8,128)}), f32[8192,512]{1,0:T(8,128)}) %all-gather.6.cloned.1.call-update) | async-done | bytes 16777232 | tf_op jit(solution)/shard_map/all_gather | solution.py:91
  383.3 7.9 %reduce_sum.22 = f32[512,512]{1,0:T(8,128)S(1)} reduce(f32[16,512,512]{2,1,0:T(8,128)} %bitcast.48, f32[]{:T(128)} %constant.51.clone.1), dimensions={0}, to_apply=%region_4.6 | reduce | flops 3932160 | bytes 17825796 | tf_op jit(solution)/shard_map/reduce_sum | solution.py:91
  391.4 1.0 fusion.42
  (54 shorter events, 2.5 us)
Async XLA Ops:
  7.2 20.4 %copy-start = (bf16[16,128,128]{2,1,0:T(8,128)(2,1)S(1)}, bf16[16,128,128]{2,1,0:T(8,128)(2,1)}, u32[]{:S(2)}) copy-start(bf16[16,128,128]{2,1,0:T(8,128)(2,1)} %param.24) | copy-start | bytes 1572868
  10.2 15.6 %all-to-all-start = ((s32[16,1,2]{2,1,0:T(1,128)}), s32[16,1,2]{2,1,0:T(1,128)S(1)}, u32[]{:S(2)}, u32[]{:S(2)}) async-start(s32[16,1,2]{2,1,0:T(1,128)} %bitcast.5), calls=%async_computation | async-start | bytes 16384 | tf_op jit(solution)/shard_map/all_to_all | solution.py:33
  53.9 4.1 %copy-start.14 = (s32[8]{0:T(128)S(1)}, s32[8]{0:T(128)}, u32[]{:S(2)}) copy-start(s32[8]{0:T(128)} %param.18) | copy-start | bytes 100
  53.9 4.1 %copy-start.3 = (bf16[1024,256]{1,0:T(8,128)(2,1)S(1)}, bf16[1024,256]{1,0:T(8,128)(2,1)}, u32[]{:S(2)}) copy-start(bf16[1024,256]{1,0:T(8,128)(2,1)} %param.14) | copy-start | bytes 1572868
  53.9 5.5 %copy-start.7 = (bf16[8,128,128]{2,1,0:T(8,128)(2,1)S(1)}, bf16[8,128,128]{2,1,0:T(8,128)(2,1)}, u32[]{:S(2)}) copy-start(bf16[8,128,128]{2,1,0:T(8,128)(2,1)} %param.20) | copy-start | bytes 786436
  53.9 46.1 %all-to-all-start.1 = ((bf16[16,2,32768]{2,1,0:T(2,128)(2,1)}), bf16[16,2,32768]{2,1,0:T(2,128)(2,1)S(1)}, u32[]{:S(2)}, u32[]{:S(2)}) async-start(bf16[16,2,32768]{2,1,0:T(2,128)(2,1)} %reshape.227), calls=%async_computation.1 | async-start | bytes 4194304 | tf_op jit(solution)/shard_map/all_to_all | solution.py:32
  57.7 81.2 %reduce-scatter.2.cloned.1.call-start = ((), (), s32[]{:S(2)}) async-start(), calls=%async_computation.4 | async-start | bytes 1572864 | tf_op jit(solution)/shard_map/reduce_scatter | solution.py:82
  61.9 4.5 %copy-start.11 = (s32[1024]{0:T(1024)S(1)}, s32[1024]{0:T(1024)}, u32[]{:S(2)}) copy-start(s32[1024]{0:T(1024)} %param.17) | copy-start | bytes 12292
  64.4 1.9 copy-start.9
  64.4 2.7 copy-start.10
  64.4 3.4 copy-start.12
  123.5 15.5 %copy-start.8 = (bf16[1024,256]{1,0:T(8,128)(2,1)S(1)}, bf16[1024,256]{1,0:T(8,128)(2,1)}, u32[]{:S(2)}) copy-start(bf16[1024,256]{1,0:T(8,128)(2,1)} %param.25) | copy-start | bytes 1572868
  126.3 25.3 %all-gather.4.cloned.1.call-start = ((), (), s32[]{:S(2)}) async-start(), calls=%async_computation.5 | async-start | bytes 1572864 | tf_op jit(solution)/shard_map/all_gather | solution.py:87
  141.5 241.8 %all-gather.6.cloned.1.call-start = ((), (), s32[]{:S(2)}) async-start(), calls=%async_computation.6 | async-start | bytes 17825792 | tf_op jit(solution)/shard_map/all_gather | solution.py:91
  162.0 1.3 copy-start.1
  163.5 0.8 copy-start.4
  177.2 7.0 %copy-start.5 = (bf16[1024,256]{1,0:T(8,128)(2,1)S(1)}, bf16[1024,256]{1,0:T(8,128)(2,1)}, u32[]{:S(2)}) copy-start(bf16[1024,256]{1,0:T(8,128)(2,1)} %copy-done.4) | copy-start | bytes 1572868
  177.2 72.1 %all-to-all-start.2 = ((bf16[16,2,32768]{2,1,0:T(2,128)(2,1)}), bf16[16,2,32768]{2,1,0:T(2,128)(2,1)S(1)}, u32[]{:S(2)}, u32[]{:S(2)}) async-start(bf16[16,2,32768]{2,1,0:T(2,128)(2,1)} %reshape.229), calls=%async_computation.3 | async-start | bytes 4194304 | tf_op jit(solution)/shard_map/all_to_all | solution.py:103
  275.4 2.0 copy-start.13
  277.4 2.5 copy-start.6
  279.9 4.0 copy-start.2
Sparse Core Ops, SparseCore 0:
  126.4 12.4 reduce-scatter.1
  141.6 9.9 all-gather.3
  154.7 228.5 all-gather.5
